TPU v7x, 32 devices: a whole 2x2x4 slice. The times are simulated.
32 devices in a mesh: row: 4 (over z), col: 8 (over y, x, core).
Axes of the slice: x: 2, y: 2, z: 4, core: 2. Of those that a mesh axis runs over, the one named last changes fastest.
Arguments:
- operator: float32 [4096, 4096], P('row', 'col'), may hold values from -0.09375 to 0.09375
- vectors: float32 [4096, 256], P('row', 'col'), may hold values from -6 to 6
- owner_map: int32 [2816, 1], P(('row', 'col')), may hold values from 0 to 7; in each aligned block of 88 rows (0 to 87, 88 to 175, ...) at most 32 rows name the same one
- coupling: float32 [4, 256, 256], P('row', 'col'), may hold values from -0.375 to 0.375
- ancestors: int32 [4, 8, 512], P('row', 'col'), may hold values from 0 to 511, as said below
- leaf_modes: float32 [4, 8, 2048, 256], P('row', 'col'), may hold values from -0.375 to 0.375
- constraint_modes: float32 [4, 8, 2048, 512], P('row', 'col'), may hold values from -0.25 to 0.25
Outputs:
- separators: float32 [4, 256, 256], P('row', 'col')
- interiors: float32 [4, 8, 2048, 256], P('row', 'col')
Inputs may be any that keep to these rules, and one draw needn't show every extreme that they name: `owner_map`: in each aligned block of 88 rows no leaf is named more than 32 times, a bound that some block reaches. `ancestors`: the 512 indices of one leaf are distinct.
All inputs are finite; a program needn't handle non-finite values.
Results may differ from a plain program's by a relative error of at most 0.00007.
Values sent between devices are 32-bit elements; how exact they have to be, the bound alone decides.
No kernel may reach another device: no remote copies, remote signals or barrier semaphores. Data moves between devices by JAX's collectives and lax.ppermute only.
A program may use at most 64 MiB of HBM per device.

v0:
```python
import jax
import jax.numpy as jnp
from jax import lax
from jax.sharding import PartitionSpec as P

highest = lax.Precision.HIGHEST


def slot_ranks(owned_rows, fanout):
    onehot = (owned_rows[..., None] == jnp.arange(fanout, dtype=jnp.int32)).astype(jnp.int32)
    running = jnp.cumsum(onehot, axis=-2)
    return jnp.sum(running * onehot, axis=-1) - 1


def on_device(operator, vectors, owner_map, coupling, ancestors, leaf_modes, constraint_modes):
    fanout = lax.axis_size("col")
    mode_local = owner_map.shape[0]
    separator_local = coupling.shape[1]
    mode_count = leaf_modes.shape[3]
    slot_count = mode_count // fanout
    mode_matrix = leaf_modes[0, 0]
    partial_adjoint = lax.dot_general(
        operator,
        lax.all_gather(vectors, "col", axis=1, tiled=True),
        (((0,), (0,)), ((), ())),
        precision=highest,
        preferred_element_type=jnp.float32,
    )
    shares = lax.psum_scatter(partial_adjoint, "row", scatter_dimension=0, tiled=True)
    forward = jnp.dot(
        operator,
        lax.all_gather(shares, "row", axis=0, tiled=True),
        precision=highest,
        preferred_element_type=jnp.float32,
    )
    vector_count = forward.shape[1]
    local_rows = lax.psum_scatter(forward, "col", scatter_dimension=0, tiled=True)
    mode_rows = local_rows[:mode_local]
    separator_raw = local_rows[mode_local : mode_local + separator_local]
    top_local = local_rows[mode_local + separator_local :]
    owned_here = owner_map[:, 0]
    target = owned_here * slot_count + slot_ranks(owned_here, fanout)
    source = (
        jnp.full((fanout * slot_count,), mode_local, jnp.int32)
        .at[target]
        .set(jnp.arange(mode_local, dtype=jnp.int32))
    )
    outgoing = jnp.take(mode_rows, source, axis=0, mode="fill", fill_value=0.0).reshape(
        fanout, slot_count, vector_count
    )
    received = lax.all_to_all(outgoing, "col", split_axis=0, concat_axis=0, tiled=True)
    flattened = received.reshape(mode_count, received.shape[2])
    modal_sum = jnp.dot(
        mode_matrix, flattened, precision=highest, preferred_element_type=jnp.float32
    )
    top_gathered = lax.all_gather(top_local, ("row", "col"), axis=0, tiled=True)
    separators = separator_raw + jnp.dot(
        coupling[0], top_gathered, precision=highest, preferred_element_type=jnp.float32
    )
    separator_all = lax.all_gather(separators, "col", axis=0, tiled=True)
    candidates = jnp.concatenate([top_gathered, separator_all], axis=0)
    picked = jnp.take(candidates, ancestors[0, 0], axis=0)
    interiors = modal_sum + jnp.dot(
        constraint_modes[0, 0], picked, precision=highest, preferred_element_type=jnp.float32
    )
    return (separators[None], interiors[None, None])


def solution(mesh):
    in_specs = (
        P("row", "col"),
        P("row", "col"),
        P(("row", "col"), None),
        P("row", "col", None),
        P("row", "col", None),
        P("row", "col", None, None),
        P("row", "col", None, None),
    )
    out_specs = (P("row", "col", None), P("row", "col", None, None))
    return jax.shard_map(
        on_device, mesh=mesh, in_specs=in_specs, out_specs=out_specs, check_vma=False
    )
```

profile of v0, /device:TPU:0, one launch (start us, length us, event | category | flops | bytes accessed | tf_op | source)
XLA Modules:
  0.0 207.7 jit_solution(3780985953271571062)
XLA Ops:
  7.2 0.0 copy-start
  7.2 0.0 all-gather.2.cloned.1.call-start
  7.2 0.7 all-gather.2.cloned.1.call-update
  7.9 0.0 reduce-scatter.3.cloned.1.call-start
  8.0 28.0 %all-gather.2.cloned.1.call-done = f32[1024,256]{0,1:T(8,128)} async-done(((f32[1024,32]{0,1:T(8,128)}), f32[1024,256]{0,1:T(8,128)}) %all-gather.2.cloned.1.call-update) | async-done | bytes 1048592 | tf_op jit(solution)/shard_map/all_gather | solution.py:24
  36.0 6.1 %fusion.14 = f32[512,256]{1,0:T(8,128)} fusion(f32[1024,512]{1,0:T(8,128)} %param.7, f32[1024,256]{0,1:T(8,128)} %all-gather.2.cloned.1.call-done), kind=kOutput, calls=%fused_computation.33 | convolution fusion | flops 1610612736 | bytes 3670016 | tf_op jit(solution)/shard_map/dot_general | solution.py:22
  42.1 0.0 reduce-scatter.3.cloned.1.call-update
  42.1 0.0 reduce-scatter.5.cloned.1.call-start
  42.2 21.9 %reduce-scatter.3.cloned.1.call-done = f32[128,256]{1,0:T(8,128)} async-done(((f32[512,256]{1,0:T(8,128)}), f32[128,256]{1,0:T(8,128)}) %reduce-scatter.3.cloned.1.call-update) | async-done | bytes 131088 | tf_op jit(solution)/shard_map/reduce_scatter | solution.py:29
  64.1 15.6 %all_gather.13 = f32[512,256]{1,0:T(8,128)S(1)} all-gather(f32[128,256]{1,0:T(8,128)} %reduce-scatter.3.cloned.1.call-done), channel_id=1, replica_groups=mesh['row'=4,'col'=8] {'row'}, dimensions={0}, use_global_device_ids=true | all-gather | bytes 655360 | tf_op jit(solution)/shard_map/all_gather | solution.py:32
  79.6 0.0 copy-start.4
  79.7 0.0 copy-start.3
  79.7 6.1 %convolution_bitcast_fusion = f32[1024,256]{0,1:T(8,128)} fusion(f32[512,256]{1,0:T(8,128)S(1)} %all_gather.13, f32[1024,512]{1,0:T(8,128)} %param.7), kind=kOutput, calls=%fused_computation.8 | convolution fusion | flops 1610612736 | bytes 3670016 | tf_op jit(solution)/shard_map/dot_general | solution.py:30
  85.7 0.0 reduce-scatter.5.cloned.1.call-update
  85.8 0.0 copy-done.4
  85.8 0.1 fusion.8
  85.9 0.1 reduce_window_sum.11
  86.0 0.2 select_reduce_fusion
  86.2 0.8 scatter_custom_fusion
  87.1 0.1 broadcast_in_dim.37
  87.1 0.0 copy-done.3
  87.2 33.1 %reduce-scatter.5.cloned.1.call-done = f32[128,256]{0,1:T(8,128)} async-done(((f32[1024,256]{0,1:T(8,128)}), f32[128,256]{0,1:T(8,128)}) %reduce-scatter.5.cloned.1.call-update) | async-done | bytes 131088 | tf_op jit(solution)/shard_map/reduce_scatter | solution.py:37
  120.3 0.0 copy-start.1
  120.3 0.0 copy-start.2
  120.3 1.1 copy.21
  121.4 1.0 slice.17
  122.4 0.1 copy.19
  122.4 1.0 gather_fusion
  123.4 0.8 broadcast_select_fusion
  124.2 3.4 %all-to-all-start = ((f32[8,32,256]{2,1,0:T(8,128)}), f32[8,32,256]{2,1,0:T(8,128)S(1)}, u32[]{:S(2)}, u32[]{:S(2)}) async-start(f32[8,32,256]{2,1,0:T(8,128)} %broadcast_select_fusion), calls=%async_computation.2 | async-start | bytes 524288 | tf_op jit(solution)/shard_map/all_to_all | solution.py:51
  127.6 42.6 %all_gather.14 = f32[256,256]{1,0:T(8,128)S(1)} all-gather(f32[8,256]{1,0:T(8,128)S(1)} %copy.19), channel_id=1, replica_groups=mesh['row'=4,'col'=8] {'row','col'}, dimensions={0}, use_global_device_ids=true | all-gather | bytes 270336 | tf_op jit(solution)/shard_map/all_gather | solution.py:56
  170.2 0.0 copy-done.1
  170.2 0.0 copy-done.2
  170.2 0.6 fusion.4
  170.8 0.1 copy.22
  170.9 0.7 copy.23
  171.6 8.3 %all_gather.15 = f32[256,256]{1,0:T(8,128)S(1)} all-gather(f32[32,256]{1,0:T(8,128)S(1)} %copy.22), channel_id=1, replica_groups=mesh['row'=4,'col'=8] {'col'}, dimensions={0}, use_global_device_ids=true | all-gather | bytes 294912 | tf_op jit(solution)/shard_map/all_gather | solution.py:60
  179.9 1.6 gather_fusion.1
  181.5 10.4 %fusion = f32[256,2048]{1,0:T(8,128)} fusion(f32[1,1,2048,512]{3,2,1,0:T(8,128)} %param.13, f32[512,256]{1,0:T(8,128)S(1)} %gather_fusion.1, pred[512]{0:T(512)(128)(4,1)S(1)} %compare_and_fusion), kind=kOutput, calls=%fused_computation.3 | convolution fusion | flops 3221356544 | bytes 6816256 | tf_op jit(solution)/shard_map/dot_general | solution.py:63
  191.9 0.0 all-to-all-done
  191.9 0.0 copy-done
  191.9 6.4 %fusion.2 = f32[1,1,2048,256]{2,3,1,0:T(8,128)} fusion(f32[256,2048]{1,0:T(8,128)} %fusion, f32[256,256]{1,0:T(8,128)S(1)} %bitcast.43, f32[1,1,2048,256]{3,2,1,0:T(8,128)S(1)} %copy-done), kind=kOutput, calls=%fused_computation.6 | convolution fusion | flops 1611137024 | bytes 6553600 | tf_op jit(solution)/shard_map/dot_general | solution.py:53
  198.3 2.9 %copy.24 = f32[1,1,2048,256]{3,2,1,0:T(8,128)} copy(f32[1,1,2048,256]{2,3,1,0:T(8,128)} %fusion.2) | data formatting | bytes 4194304
  (9 shorter events, 0.1 us)
Async XLA Ops:
  7.2 184.7 %copy-start = (f32[1,1,2048,256]{3,2,1,0:T(8,128)S(1)}, f32[1,1,2048,256]{3,2,1,0:T(8,128)}, u32[]{:S(2)}) copy-start(f32[1,1,2048,256]{3,2,1,0:T(8,128)} %param.12) | copy-start | bytes 6291460
  7.2 28.8 %all-gather.2.cloned.1.call-start = ((), (), s32[]{:S(2)}) async-start(), calls=%async_computation.3 | async-start | bytes 1179648 | tf_op jit(solution)/shard_map/all_gather | solution.py:24
  7.9 56.2 %reduce-scatter.3.cloned.1.call-start = ((), (), s32[]{:S(2)}) async-start(), calls=%async_computation.4 | async-start | bytes 655360 | tf_op jit(solution)/shard_map/reduce_scatter | solution.py:29
  42.1 78.2 %reduce-scatter.5.cloned.1.call-start = ((), (), s32[]{:S(2)}) async-start(), calls=%async_computation.5 | async-start | bytes 1179648 | tf_op jit(solution)/shard_map/reduce_scatter | solution.py:37
  79.6 6.1 %copy-start.4 = (s32[88,1]{0,1:T(1,128)S(1)}, s32[88,1]{0,1:T(1,128)}, u32[]{:S(2)}) copy-start(s32[88,1]{0,1:T(1,128)} %param.9) | copy-start | bytes 1060
  79.7 7.5 %copy-start.3 = (s32[1,1,512]{2,1,0:T(1,128)S(1)}, s32[1,1,512]{2,1,0:T(1,128)}, u32[]{:S(2)}) copy-start(s32[1,1,512]{2,1,0:T(1,128)} %param.11) | copy-start | bytes 6148
  120.3 49.9 %copy-start.1 = (f32[128,256]{0,1:T(8,128)S(1)}, f32[128,256]{0,1:T(8,128)}, u32[]{:S(2)}) copy-start(f32[128,256]{0,1:T(8,128)} %reduce-scatter.5.cloned.1.call-done) | copy-start | bytes 393220
  120.3 49.9 %copy-start.2 = (f32[1,32,256]{2,1,0:T(8,128)S(1)}, f32[1,32,256]{2,1,0:T(8,128)}, u32[]{:S(2)}) copy-start(f32[1,32,256]{2,1,0:T(8,128)} %param.10) | copy-start | bytes 98308
  124.2 67.7 %all-to-all-start = ((f32[8,32,256]{2,1,0:T(8,128)}), f32[8,32,256]{2,1,0:T(8,128)S(1)}, u32[]{:S(2)}, u32[]{:S(2)}) async-start(f32[8,32,256]{2,1,0:T(8,128)} %broadcast_select_fusion), calls=%async_computation.2 | async-start | bytes 524288 | tf_op jit(solution)/shard_map/all_to_all | solution.py:51
Sparse Core Ops, SparseCore 0:
  9.9 26.0 all-gather.1
  42.2 21.8 reduce-scatter.2
  85.9 34.3 reduce-scatter.4
where the time goes:
time: 208 us
  waiting for transfers between devices  83.8 us (40%)
  blocking collectives  66.5 us (32%)
  matrix products  29.5 us (14%)
  between operations  13.9 us (7%)
  local copies, waits for them, and re-layouts  9.27 us (4%)
  starting transfers between devices  3.53 us (2%)
    all_gather x1, blocking collectives, on_device(): top_gathered = lax.all_gather(top_local, ('row', 'col'), axis=0, tiled=True)  42.6 us
    reduce_scatter x1, waiting for transfers between devices, on_device(): lax.psum_scatter(forward, 'col', scatter_dimension=0, tiled=True)  33.1 us
    all_gather x1, waiting for transfers between devices, on_device(): lax.all_gather(vectors, 'col', axis=1, tiled=True)  28 us
    reduce_scatter x1, waiting for transfers between devices, on_device(): lax.psum_scatter(partial_adjoint, 'row', scatter_dimension=0, tiled=True)  21.9 us
    all_gather x1, blocking collectives, on_device(): lax.all_gather(shares, 'row', axis=0, tiled=True)  15.6 us
    dot_general x1, matrix products, on_device(): jnp.dot(constraint_modes[0, 0], picked, precision=highest, preferred_elem...  10.4 us
    all_gather x1, blocking collectives, on_device(): separator_all = lax.all_gather(separators, 'col', axis=0, tiled=True)  8.28 us
    dot_general x1, matrix products, on_device(): jnp.dot(mode_matrix, flattened, precision=highest, preferred_element_type...  6.4 us
  transfers between devices with their start and end apart: 4, of which 3 were waited for; matrix products, arithmetic and copies ran while one was open for 7% of the time, Pallas kernels for 0%

commit v1 on v0

--- a/solution.py
+++ b/solution.py
@@ -4,6 +4,27 @@
 from jax.sharding import PartitionSpec as P
 
 highest = lax.Precision.HIGHEST
+
+
+def collect(x, axis, dim):
+    size, index, extent = (lax.axis_size(axis), lax.axis_index(axis), x.shape[dim])
+    upward = [(i, (i + 1) % size) for i in range(size)]
+    left = [(i, (i - 1) % size) for i in range(size)]
+    whole = jnp.zeros((*x.shape[:dim], size * extent, *x.shape[dim + 1 :]), x.dtype)
+    whole = lax.dynamic_update_slice_in_dim(whole, x, index * extent, axis=dim)
+    from_left = from_right = x
+    middle = size // 2
+    for lap in range(1, middle + 1):
+        from_left = lax.ppermute(from_left, axis, upward)
+        whole = lax.dynamic_update_slice_in_dim(
+            whole, from_left, (index - lap) % size * extent, axis=dim
+        )
+        if lap < size - middle:
+            from_right = lax.ppermute(from_right, axis, left)
+            whole = lax.dynamic_update_slice_in_dim(
+                whole, from_right, (index + lap) % size * extent, axis=dim
+            )
+    return whole
 
 
 def slot_ranks(owned_rows, fanout):
@@ -21,7 +42,7 @@
     mode_matrix = leaf_modes[0, 0]
     partial_adjoint = lax.dot_general(
         operator,
-        lax.all_gather(vectors, "col", axis=1, tiled=True),
+        collect(vectors, "col", 1),
         (((0,), (0,)), ((), ())),
         precision=highest,
         preferred_element_type=jnp.float32,

time: 208 us -> 201 us (0.966)
  waiting for transfers between devices: 83.8 us -> 71.3 us
  starting transfers between devices: 3.53 us -> 12.4 us
  matrix products: 29.5 us -> 24.6 us
    all_gather x1 -> x0, waiting for transfers between devices: 28 us -> none  [on_device(): lax.all_gather(vectors, 'col', axis=1, tiled=True)]
    ppermute x0 -> x7, waiting for transfers between devices: none -> 15.3 us  [the longest x4 10.7 us: collect(): from_left = lax.ppermute(from_left, axis, upward)]
    ppermute x0 -> x7, starting transfers between devices: none -> 8.89 us  [the longest x3 8.88 us: collect(): from_right = lax.ppermute(from_right, axis, left)]
    dot_general x1, matrix products: 6.07 us -> 2.73 us  [on_device(): lax.dot_general(operator, collect(vectors, 'col', 1), (((0,), (0,)), ((),...]
  transfers between devices with their start and end apart: 4 -> 10, of which waited for: 3 -> 7; matrix products, arithmetic and copies ran while one was open for 7% -> 8% of each run, Pallas kernels for 0% -> 0%
where the time goes in v1:
time: 201 us
  waiting for transfers between devices  71.3 us (35%)
  blocking collectives  66.4 us (33%)
  matrix products  24.6 us (12%)
  between operations  14.2 us (7%)
  starting transfers between devices  12.4 us (6%)
  local copies, waits for them, and re-layouts  10.5 us (5%)
    all_gather x1, blocking collectives, on_device(): top_gathered = lax.all_gather(top_local, ('row', 'col'), axis=0, tiled=True)  42.6 us
    reduce_scatter x1, waiting for transfers between devices, on_device(): lax.psum_scatter(forward, 'col', scatter_dimension=0, tiled=True)  33.1 us
    reduce_scatter x1, waiting for transfers between devices, on_device(): lax.psum_scatter(partial_adjoint, 'row', scatter_dimension=0, tiled=True)  22.8 us
    all_gather x1, blocking collectives, on_device(): lax.all_gather(shares, 'row', axis=0, tiled=True)  15.6 us
    ppermute x4, waiting for transfers between devices, collect(): from_left = lax.ppermute(from_left, axis, upward)  10.7 us
    dot_general x1, matrix products, on_device(): jnp.dot(constraint_modes[0, 0], picked, precision=highest, preferred_elem...  10.4 us
    ppermute x3, starting transfers between devices, collect(): from_right = lax.ppermute(from_right, axis, left)  8.88 us
    all_gather x1, blocking collectives, on_device(): separator_all = lax.all_gather(separators, 'col', axis=0, tiled=True)  8.28 us
  transfers between devices with their start and end apart: 10, of which 7 were waited for; matrix products, arithmetic and copies ran while one was open for 8% of the time, Pallas kernels for 0%

profile of v1, /device:TPU:0, one launch (start us, length us, event | category | flops | bytes accessed | tf_op | source)
XLA Modules:
  0.0 200.7 jit_solution(2961152753010612017)
XLA Ops:
  7.2 0.0 copy-start
  7.2 0.0 reduce-scatter.3.cloned.1.call-start
  7.2 3.4 %collective-permute-start.1 = (f32[1024,32]{0,1:T(8,128)}, f32[1024,32]{0,1:T(8,128)S(1)}, u32[]{:S(2)}, u32[]{:S(2)}) collective-permute-start(f32[1024,32]{0,1:T(8,128)} %param.8), channel_id=1, source_target_pairs={{0,7},{1,0},{2,1},{3,2},{4,3},{5,4},{6,5},{7,6},{8,15},{9,8},{10,9... | collective-permute-start | bytes 393224 | tf_op jit(solution)/shard_map/ppermute | solution.py:23
  10.6 0.0 collective-permute-start
  10.6 0.0 copy-start.1
  10.6 0.1 broadcast_in_dim.38
  10.8 1.0 constant_dynamic-update-slice_fusion.7
  11.8 2.1 %collective-permute-done.1 = f32[1024,32]{0,1:T(8,128)S(1)} collective-permute-done((f32[1024,32]{0,1:T(8,128)}, f32[1024,32]{0,1:T(8,128)S(1)}, u32[]{:S(2)}, u32[]{:S(2)}) %collective-permute-start.1) | collective-permute-done | bytes 131104 | tf_op jit(solution)/shard_map/ppermute | solution.py:23
  13.9 2.7 %collective-permute-start.3 = (f32[1024,32]{0,1:T(8,128)S(1)}, f32[1024,32]{0,1:T(8,128)S(1)}, u32[]{:S(2)}, u32[]{:S(2)}) collective-permute-start(f32[1024,32]{0,1:T(8,128)S(1)} %collective-permute-done.1), channel_id=1, source_target_pairs={{0,7},{1,0},{2,1},{3,2},{4,3},{5,4},{6,5},{7,6},{8,15},{9,8},{10,9... | collective-permute-start | bytes 393224 | tf_op jit(solution)/shard_map/ppermute | solution.py:23
  16.6 0.0 collective-permute-done
  16.6 0.0 collective-permute-start.2
  16.7 2.5 %collective-permute-done.3 = f32[1024,32]{0,1:T(8,128)S(1)} collective-permute-done((f32[1024,32]{0,1:T(8,128)S(1)}, f32[1024,32]{0,1:T(8,128)S(1)}, u32[]{:S(2)}, u32[]{:S(2)}) %collective-permute-start.3) | collective-permute-done | bytes 131104 | tf_op jit(solution)/shard_map/ppermute | solution.py:23
  19.2 2.8 %collective-permute-start.5 = (f32[1024,32]{0,1:T(8,128)S(1)}, f32[1024,32]{0,1:T(8,128)S(1)}, u32[]{:S(2)}, u32[]{:S(2)}) collective-permute-start(f32[1024,32]{0,1:T(8,128)S(1)} %collective-permute-done.3), channel_id=1, source_target_pairs={{0,7},{1,0},{2,1},{3,2},{4,3},{5,4},{6,5},{7,6},{8,15},{9,8},{10,9... | collective-permute-start | bytes 393224 | tf_op jit(solution)/shard_map/ppermute | solution.py:23
  21.9 0.2 collective-permute-done.2
  22.1 0.0 collective-permute-start.4
  22.2 5.2 %collective-permute-done.4 = f32[1024,32]{0,1:T(8,128)S(1)} collective-permute-done((f32[1024,32]{0,1:T(8,128)S(1)}, f32[1024,32]{0,1:T(8,128)S(1)}, u32[]{:S(2)}, u32[]{:S(2)}) %collective-permute-start.4) | collective-permute-done | bytes 131104 | tf_op jit(solution)/shard_map/ppermute | solution.py:18
  27.4 0.0 collective-permute-start.6
  27.4 0.0 collective-permute-done.5
  27.5 5.2 %collective-permute-done.6 = f32[1024,32]{0,1:T(8,128)S(1)} collective-permute-done((f32[1024,32]{0,1:T(8,128)S(1)}, f32[1024,32]{0,1:T(8,128)S(1)}, u32[]{:S(2)}, u32[]{:S(2)}) %collective-permute-start.6) | collective-permute-done | bytes 131104 | tf_op jit(solution)/shard_map/ppermute | solution.py:18
  32.7 0.0 copy-done.1
  32.7 2.7 %convolution_bitcast_fusion.1 = f32[512,256]{0,1:T(8,128)} fusion(f32[1024,256]{0,1:T(8,128)S(1)} %constant_dynamic-update-slice_fusion, f32[1024,512]{1,0:T(8,128)S(1)} %copy-done.1), kind=kOutput, calls=%fused_computation.9 | convolution fusion | flops 1610612736 | bytes 3670016 | tf_op jit(solution)/shard_map/dot_general | solution.py:43
  35.5 0.0 reduce-scatter.3.cloned.1.call-update
  35.5 0.0 reduce-scatter.5.cloned.1.call-start
  35.6 22.8 %reduce-scatter.3.cloned.1.call-done = f32[128,256]{0,1:T(8,128)} async-done(((f32[512,256]{0,1:T(8,128)}), f32[128,256]{0,1:T(8,128)}) %reduce-scatter.3.cloned.1.call-update) | async-done | bytes 131088 | tf_op jit(solution)/shard_map/reduce_scatter | solution.py:50
  58.4 15.6 %all_gather.9 = f32[512,256]{0,1:T(8,128)S(1)} all-gather(f32[128,256]{0,1:T(8,128)} %reduce-scatter.3.cloned.1.call-done), channel_id=1, replica_groups=mesh['row'=4,'col'=8] {'row'}, dimensions={0}, use_global_device_ids=true | all-gather | bytes 655360 | tf_op jit(solution)/shard_map/all_gather | solution.py:53
  73.9 0.0 copy-start.5
  73.9 0.0 copy-start.4
  73.9 4.5 %convolution_bitcast_fusion = f32[1024,256]{0,1:T(8,128)} fusion(f32[512,256]{0,1:T(8,128)S(1)} %all_gather.9, f32[1024,512]{1,0:T(8,128)} %param.7), kind=kOutput, calls=%fused_computation.8 | convolution fusion | flops 1610612736 | bytes 3670016 | tf_op jit(solution)/shard_map/dot_general | solution.py:51
  78.4 0.0 reduce-scatter.5.cloned.1.call-update
  78.5 0.0 copy-done.5
  78.5 0.1 fusion.8
  78.6 0.1 reduce_window_sum.11
  78.7 0.2 select_reduce_fusion
  78.9 0.8 scatter_custom_fusion
  79.8 0.1 broadcast_in_dim.41
  79.8 0.0 copy-done.4
  79.9 33.1 %reduce-scatter.5.cloned.1.call-done = f32[128,256]{0,1:T(8,128)} async-done(((f32[1024,256]{0,1:T(8,128)}), f32[128,256]{0,1:T(8,128)}) %reduce-scatter.5.cloned.1.call-update) | async-done | bytes 131088 | tf_op jit(solution)/shard_map/reduce_scatter | solution.py:58
  113.1 0.0 copy-start.2
  113.1 0.0 copy-start.3
  113.1 1.1 copy.21
  114.1 1.0 slice.17
  115.1 0.1 copy.19
  115.2 1.0 gather_fusion
  116.2 0.8 broadcast_select_fusion
  117.0 3.4 %all-to-all-start = ((f32[8,32,256]{2,1,0:T(8,128)}), f32[8,32,256]{2,1,0:T(8,128)S(1)}, u32[]{:S(2)}, u32[]{:S(2)}) async-start(f32[8,32,256]{2,1,0:T(8,128)} %broadcast_select_fusion), calls=%async_computation.2 | async-start | bytes 524288 | tf_op jit(solution)/shard_map/all_to_all | solution.py:72
  120.4 42.6 %all_gather.10 = f32[256,256]{1,0:T(8,128)S(1)} all-gather(f32[8,256]{1,0:T(8,128)S(1)} %copy.19), channel_id=1, replica_groups=mesh['row'=4,'col'=8] {'row','col'}, dimensions={0}, use_global_device_ids=true | all-gather | bytes 270336 | tf_op jit(solution)/shard_map/all_gather | solution.py:77
  163.0 0.0 copy-done.2
  163.0 0.0 copy-done.3
  163.0 0.6 fusion.4
  163.6 0.1 copy.22
  163.6 0.7 copy.23
  164.3 8.3 %all_gather.11 = f32[256,256]{1,0:T(8,128)S(1)} all-gather(f32[32,256]{1,0:T(8,128)S(1)} %copy.22), channel_id=1, replica_groups=mesh['row'=4,'col'=8] {'col'}, dimensions={0}, use_global_device_ids=true | all-gather | bytes 294912 | tf_op jit(solution)/shard_map/all_gather | solution.py:81
  172.6 1.6 gather_fusion.1
  174.2 10.4 %fusion = f32[256,2048]{1,0:T(8,128)} fusion(f32[1,1,2048,512]{3,2,1,0:T(8,128)} %param.13, f32[512,256]{1,0:T(8,128)S(1)} %gather_fusion.1, pred[512]{0:T(512)(128)(4,1)S(1)} %compare_and_fusion), kind=kOutput, calls=%fused_computation.3 | convolution fusion | flops 3221356544 | bytes 6816256 | tf_op jit(solution)/shard_map/dot_general | solution.py:84
  184.6 0.0 all-to-all-done
  184.6 0.0 copy-done
  184.6 6.4 %fusion.2 = f32[1,1,2048,256]{2,3,1,0:T(8,128)} fusion(f32[256,2048]{1,0:T(8,128)} %fusion, f32[256,256]{1,0:T(8,128)S(1)} %bitcast.45, f32[1,1,2048,256]{3,2,1,0:T(8,128)S(1)} %copy-done), kind=kOutput, calls=%fused_computation.6 | convolution fusion | flops 1611137024 | bytes 6553600 | tf_op jit(solution)/shard_map/dot_general | solution.py:74
  191.0 2.9 %copy.24 = f32[1,1,2048,256]{3,2,1,0:T(8,128)} copy(f32[1,1,2048,256]{2,3,1,0:T(8,128)} %fusion.2) | data formatting | bytes 4194304
  (16 shorter events, 0.2 us)
Async XLA Ops:
  7.2 177.4 %copy-start = (f32[1,1,2048,256]{3,2,1,0:T(8,128)S(1)}, f32[1,1,2048,256]{3,2,1,0:T(8,128)}, u32[]{:S(2)}) copy-start(f32[1,1,2048,256]{3,2,1,0:T(8,128)} %param.12) | copy-start | bytes 6291460
  7.2 51.2 %reduce-scatter.3.cloned.1.call-start = ((), (), s32[]{:S(2)}) async-start(), calls=%async_computation.3 | async-start | bytes 655360 | tf_op jit(solution)/shard_map/reduce_scatter | solution.py:50
  7.2 6.7 %collective-permute-start.1 = (f32[1024,32]{0,1:T(8,128)}, f32[1024,32]{0,1:T(8,128)S(1)}, u32[]{:S(2)}, u32[]{:S(2)}) collective-permute-start(f32[1024,32]{0,1:T(8,128)} %param.8), channel_id=1, source_target_pairs={{0,7},{1,0},{2,1},{3,2},{4,3},{5,4},{6,5},{7,6},{8,15},{9,8},{10,9... | collective-permute-start | bytes 393224 | tf_op jit(solution)/shard_map/ppermute | solution.py:23
  10.6 6.0 %collective-permute-start = (f32[1024,32]{0,1:T(8,128)}, f32[1024,32]{0,1:T(8,128)S(1)}, u32[]{:S(2)}, u32[]{:S(2)}) collective-permute-start(f32[1024,32]{0,1:T(8,128)} %param.8), channel_id=1, source_target_pairs={{0,1},{1,2},{2,3},{3,4},{4,5},{5,6},{6,7},{7,0},{8,9},{9,10},{10,1... | collective-permute-start | bytes 393224 | tf_op jit(solution)/shard_map/ppermute | solution.py:18
  10.6 22.1 %copy-start.1 = (f32[1024,512]{1,0:T(8,128)S(1)}, f32[1024,512]{1,0:T(8,128)}, u32[]{:S(2)}) copy-start(f32[1024,512]{1,0:T(8,128)} %param.7) | copy-start | bytes 6291460
  13.9 5.2 %collective-permute-start.3 = (f32[1024,32]{0,1:T(8,128)S(1)}, f32[1024,32]{0,1:T(8,128)S(1)}, u32[]{:S(2)}, u32[]{:S(2)}) collective-permute-start(f32[1024,32]{0,1:T(8,128)S(1)} %collective-permute-done.1), channel_id=1, source_target_pairs={{0,7},{1,0},{2,1},{3,2},{4,3},{5,4},{6,5},{7,6},{8,15},{9,8},{10,9... | collective-permute-start | bytes 393224 | tf_op jit(solution)/shard_map/ppermute | solution.py:23
  16.6 5.5 %collective-permute-start.2 = (f32[1024,32]{0,1:T(8,128)S(1)}, f32[1024,32]{0,1:T(8,128)S(1)}, u32[]{:S(2)}, u32[]{:S(2)}) collective-permute-start(f32[1024,32]{0,1:T(8,128)S(1)} %collective-permute-done), channel_id=1, source_target_pairs={{0,1},{1,2},{2,3},{3,4},{4,5},{5,6},{6,7},{7,0},{8,9},{9,10},{10,1... | collective-permute-start | bytes 393224 | tf_op jit(solution)/shard_map/ppermute | solution.py:18
  19.2 8.3 %collective-permute-start.5 = (f32[1024,32]{0,1:T(8,128)S(1)}, f32[1024,32]{0,1:T(8,128)S(1)}, u32[]{:S(2)}, u32[]{:S(2)}) collective-permute-start(f32[1024,32]{0,1:T(8,128)S(1)} %collective-permute-done.3), channel_id=1, source_target_pairs={{0,7},{1,0},{2,1},{3,2},{4,3},{5,4},{6,5},{7,6},{8,15},{9,8},{10,9... | collective-permute-start | bytes 393224 | tf_op jit(solution)/shard_map/ppermute | solution.py:23
  22.1 5.3 %collective-permute-start.4 = (f32[1024,32]{0,1:T(8,128)S(1)}, f32[1024,32]{0,1:T(8,128)S(1)}, u32[]{:S(2)}, u32[]{:S(2)}) collective-permute-start(f32[1024,32]{0,1:T(8,128)S(1)} %collective-permute-done.2), channel_id=1, source_target_pairs={{0,1},{1,2},{2,3},{3,4},{4,5},{5,6},{6,7},{7,0},{8,9},{9,10},{10,1... | collective-permute-start | bytes 393224 | tf_op jit(solution)/shard_map/ppermute | solution.py:18
  27.4 5.3 %collective-permute-start.6 = (f32[1024,32]{0,1:T(8,128)S(1)}, f32[1024,32]{0,1:T(8,128)S(1)}, u32[]{:S(2)}, u32[]{:S(2)}) collective-permute-start(f32[1024,32]{0,1:T(8,128)S(1)} %collective-permute-done.4), channel_id=1, source_target_pairs={{0,1},{1,2},{2,3},{3,4},{4,5},{5,6},{6,7},{7,0},{8,9},{9,10},{10,1... | collective-permute-start | bytes 393224 | tf_op jit(solution)/shard_map/ppermute | solution.py:18
  35.5 77.5 %reduce-scatter.5.cloned.1.call-start = ((), (), s32[]{:S(2)}) async-start(), calls=%async_computation.4 | async-start | bytes 1179648 | tf_op jit(solution)/shard_map/reduce_scatter | solution.py:58
  73.9 4.5 %copy-start.5 = (s32[88,1]{0,1:T(1,128)S(1)}, s32[88,1]{0,1:T(1,128)}, u32[]{:S(2)}) copy-start(s32[88,1]{0,1:T(1,128)} %param.9) | copy-start | bytes 1060
  73.9 5.9 %copy-start.4 = (s32[1,1,512]{2,1,0:T(1,128)S(1)}, s32[1,1,512]{2,1,0:T(1,128)}, u32[]{:S(2)}) copy-start(s32[1,1,512]{2,1,0:T(1,128)} %param.11) | copy-start | bytes 6148
  113.1 49.9 %copy-start.2 = (f32[128,256]{0,1:T(8,128)S(1)}, f32[128,256]{0,1:T(8,128)}, u32[]{:S(2)}) copy-start(f32[128,256]{0,1:T(8,128)} %reduce-scatter.5.cloned.1.call-done) | copy-start | bytes 393220
  113.1 49.9 %copy-start.3 = (f32[1,32,256]{2,1,0:T(8,128)S(1)}, f32[1,32,256]{2,1,0:T(8,128)}, u32[]{:S(2)}) copy-start(f32[1,32,256]{2,1,0:T(8,128)} %param.10) | copy-start | bytes 98308
  117.0 67.6 %all-to-all-start = ((f32[8,32,256]{2,1,0:T(8,128)}), f32[8,32,256]{2,1,0:T(8,128)S(1)}, u32[]{:S(2)}, u32[]{:S(2)}) async-start(f32[8,32,256]{2,1,0:T(8,128)} %broadcast_select_fusion), calls=%async_computation.2 | async-start | bytes 524288 | tf_op jit(solution)/shard_map/all_to_all | solution.py:72
Sparse Core Ops, SparseCore 0:
  35.6 22.7 reduce-scatter.2
  78.6 34.4 reduce-scatter.4
